TPU v7x, 128 devices: a whole 4x4x4 slice. The times are simulated.
128 devices in a mesh: dp: 16 (over y_hi, z, core), cache: 8 (over y_lo, x).
Axes of the slice: x: 4, y: 4 (y_hi: 2, y_lo: 2; y = y_hi * 2 + y_lo), z: 4, core: 2. Of those that a mesh axis runs over, the one named last changes fastest.
Arguments:
- hidden_in: bfloat16 [16384, 2560], P(('dp', 'cache')), may hold values from -6 to 6
- placing: int32 [16384], P('dp'), may hold values from 0 to 16383, as said below
- prompt_start: int32 [16384], P(('dp', 'cache')), may hold values from 0 to 16383, as said below
- attn_gain: float32 [2560], replicated, may hold values from 0.5 to 1.5
- w_qkv: bfloat16 [2560, 1792], P(('dp', 'cache'))
- w_out: bfloat16 [1280, 2560], P(('dp', 'cache')), may hold values from -0.15625 to 0.15625
- moe_gain: float32 [2560], replicated, may hold values from 0.5 to 1.5
- routes: int32 [16384, 6], P(('dp', 'cache')), may hold values from 0 to 63, all different within a row; in each aligned block of 128 rows (0 to 127, 128 to 255, ...) at most 16 rows name the same one
- route_weight: float32 [16384, 6], P(('dp', 'cache')), may hold values from 0.05 to 0.35
- w_gate_up: bfloat16 [128, 2560, 1536], P(('dp', 'cache')), may hold values from -0.125 to 0.125
- w_down: bfloat16 [128, 768, 2560], P(('dp', 'cache')), may hold values from -0.15625 to 0.15625
Outputs:
- mixed: bfloat16 [16384, 2560], P(('dp', 'cache'))
- cache_keys: bfloat16 [16384, 256], P(('dp', 'cache'))
- cache_values: bfloat16 [16384, 256], P(('dp', 'cache'))
Inputs may be any that keep to these rules, and one draw needn't show every extreme that they name: `placing`: a permutation of the 16384 positions; dealt rows g * 1024 to (g+1) * 1024 - 1 hold natural positions of the same range, and the dealt rows c * 128 + j * 16 to c * 128 + (j+1) * 16 - 1 of a group hold natural positions of its span j * 128 to (j+1) * 128 - 1. Prompts are runs of consecutive natural positions inside one group of 1024, of at most 512 tokens, some of exactly 512; prompt_start[r] <= placing[r] and it is the first position of that run. `routes`: in the rows of one device (aligned blocks of 128 rows) no expert is named more than 16 times.
All inputs are finite; a program needn't handle non-finite values.
Results may differ from a plain program's by a relative error of at most 0.014.
Values may be sent and summed in bfloat16 or wider, within the bound.
No kernel may reach another device: no remote copies, remote signals or barrier semaphores. Data moves between devices by JAX's collectives and lax.ppermute only.
A program may use at most 128 MiB of HBM per device.

v0:
```python
import jax
import jax.numpy as jnp
from jax import lax
from jax.sharding import PartitionSpec as P

HD = 128
QH = 10
KVH = 2
TOP = 6
norm_eps = 1e-05
rope_base = 500000.0
masked_score = -1e30


def rms_scaled(features, gain_vector):
    widened = features.astype(jnp.float32)
    factor = lax.rsqrt(jnp.mean(widened * widened, axis=-1, keepdims=True) + norm_eps)
    return (widened * factor * gain_vector).astype(jnp.bfloat16)


def rotated(projected, position, head_count):
    row_count = projected.shape[0]
    grouped = projected.reshape(row_count, head_count, HD)
    half_size = HD // 2
    inverse = rope_base ** (-(jnp.arange(half_size, dtype=jnp.float32) * 2.0 / HD))
    angles = position.astype(jnp.float32)[:, None] * inverse[None, :]
    cosine = jnp.cos(angles)[:, None, :]
    sine_part = jnp.sin(angles)[:, None, :]
    first_half = grouped[..., :half_size]
    second = grouped[..., half_size:]
    turned = jnp.concatenate(
        [first_half * cosine - second * sine_part, second * cosine + first_half * sine_part],
        axis=-1,
    )
    return turned.reshape(row_count, head_count * HD).astype(jnp.bfloat16)


def expert_half(slot_block, gate_up, down_part):
    flat_rows = slot_block.reshape(-1, slot_block.shape[-1])
    joined = jnp.dot(flat_rows, gate_up, preferred_element_type=jnp.float32)
    half_size = gate_up.shape[1] // 2
    active = (jax.nn.silu(joined[:, :half_size]) * joined[:, half_size:]).astype(jnp.bfloat16)
    return (
        jnp.dot(active, down_part, preferred_element_type=jnp.float32)
        .astype(jnp.bfloat16)
        .reshape(slot_block.shape)
    )


def per_device(
    hidden_in,
    placing,
    prompt_start,
    attn_gain,
    w_qkv,
    w_out,
    moe_gain,
    routes,
    route_weight,
    w_gate_up,
    w_down,
):
    row_count = hidden_in.shape[0]
    model_width = hidden_in.shape[1]
    cache_size = lax.axis_size("cache")
    my_index = lax.axis_index("cache")
    deal_rows = row_count // cache_size
    query_width = QH * HD
    kv_width = KVH * HD
    group_base = lax.axis_index("dp") * placing.shape[0]
    my_place = lax.dynamic_slice_in_dim(placing, my_index * row_count, row_count)
    position = my_place - prompt_start
    normed = rms_scaled(hidden_in, attn_gain)
    full_qkv, full_out = (
        lax.all_gather(w_qkv, ("dp", "cache"), axis=0, tiled=True),
        lax.all_gather(w_out, ("dp", "cache"), axis=0, tiled=True),
    )
    projected = jnp.dot(normed, full_qkv, preferred_element_type=jnp.float32)
    queries = rotated(projected[:, :query_width], position, QH)
    keys_here = rotated(projected[:, query_width : query_width + kv_width], position, KVH)
    values_here = projected[:, query_width + kv_width :].astype(jnp.bfloat16)
    group_size = QH // KVH
    query_heads = queries.reshape(row_count, KVH, group_size, HD)
    score_scale = HD ** (-0.5)
    highest = jnp.full((row_count, KVH, group_size), masked_score, jnp.float32)
    key_piece = lax.all_gather(keys_here, "cache", axis=0, tiled=True)
    value_piece = lax.all_gather(values_here, "cache", axis=0, tiled=True)
    piece_rows = key_piece.shape[0]
    key_heads = key_piece.reshape(piece_rows, KVH, HD)
    value_heads = value_piece.reshape(piece_rows, KVH, HD)
    scores = (
        jnp.einsum("tkgd,rkd->tkgr", query_heads, key_heads, preferred_element_type=jnp.float32)
        * score_scale
    )
    allowed = (placing[None, :] >= prompt_start[:, None]) & (placing[None, :] <= my_place[:, None])
    allowed = allowed[:, None, None, :]
    new_highest = jnp.maximum(highest, jnp.max(jnp.where(allowed, scores, masked_score), axis=-1))
    weights = jnp.where(allowed, jnp.exp(scores - new_highest[..., None]), 0.0)
    denominator = jnp.sum(weights, axis=-1)
    numerator = jnp.einsum(
        "tkgr,rkd->tkgd",
        weights.astype(jnp.bfloat16),
        value_heads,
        preferred_element_type=jnp.float32,
    )
    highest, denominator, numerator = (new_highest, denominator, numerator)
    context = (
        (numerator / denominator[..., None]).reshape(row_count, query_width).astype(jnp.bfloat16)
    )
    attn_out = jnp.dot(context, full_out, preferred_element_type=jnp.float32)
    attended = (hidden_in.astype(jnp.float32) + attn_out).astype(jnp.bfloat16)
    moe_in = rms_scaled(attended, moe_gain)
    device_count = lax.axis_size(("dp", "cache"))
    expert_count = device_count // 2
    capacity = 4 * row_count * TOP // (3 * expert_count)
    expert_ids = routes.reshape(-1)
    one_hot = (expert_ids[:, None] == jnp.arange(expert_count, dtype=jnp.int32)[None, :]).astype(
        jnp.int32
    )
    slot_rank = jnp.sum((jnp.cumsum(one_hot, axis=0) - one_hot) * one_hot, axis=1)
    slot_index = expert_ids * capacity + slot_rank
    source_row = (
        jnp.full((expert_count * capacity,), row_count, jnp.int32)
        .at[slot_index]
        .set(jnp.arange(row_count * TOP, dtype=jnp.int32) // TOP)
    )
    padded = jnp.concatenate([moe_in, jnp.zeros((1, model_width), jnp.bfloat16)], axis=0)
    outgoing = padded[source_row].reshape(expert_count, capacity, model_width)
    partial_value = expert_half(
        lax.all_to_all(
            jnp.repeat(outgoing, 2, axis=0),
            ("dp", "cache"),
            split_axis=0,
            concat_axis=0,
            tiled=True,
        ),
        w_gate_up[0],
        w_down[0],
    )
    returned = lax.all_to_all(
        partial_value, ("dp", "cache"), split_axis=0, concat_axis=0, tiled=True
    )
    halves = returned.reshape(expert_count, 2, capacity, model_width).astype(jnp.float32)
    merged = (halves[:, 0] + halves[:, 1]).astype(jnp.bfloat16)
    picked = merged.reshape(expert_count * capacity, model_width)[slot_index].reshape(
        row_count, TOP, model_width
    )
    mixture = jnp.sum(route_weight[:, :, None] * picked.astype(jnp.float32), axis=1)
    finished = (attended.astype(jnp.float32) + mixture).astype(jnp.bfloat16)
    package = (
        finished.reshape(cache_size, deal_rows, model_width),
        keys_here.reshape(cache_size, deal_rows, kv_width),
        values_here.reshape(cache_size, deal_rows, kv_width),
    )
    home_rows, home_keys, home_values = (
        lax.all_to_all(package[0], "cache", split_axis=0, concat_axis=0, tiled=True),
        lax.all_to_all(package[1], "cache", split_axis=0, concat_axis=0, tiled=True),
        lax.all_to_all(package[2], "cache", split_axis=0, concat_axis=0, tiled=True),
    )
    sender_rows = (
        jnp.arange(cache_size, dtype=jnp.int32)[:, None] * row_count
        + my_index * deal_rows
        + jnp.arange(deal_rows, dtype=jnp.int32)[None, :]
    ).reshape(-1)
    target = placing[sender_rows] - group_base - my_index * row_count
    mixed = (
        jnp.zeros((row_count, model_width), jnp.bfloat16)
        .at[target]
        .set(home_rows.reshape(-1, model_width))
    )
    cache_keys = (
        jnp.zeros((row_count, kv_width), jnp.bfloat16)
        .at[target]
        .set(home_keys.reshape(-1, kv_width))
    )
    cache_values = (
        jnp.zeros((row_count, kv_width), jnp.bfloat16)
        .at[target]
        .set(home_values.reshape(-1, kv_width))
    )
    return (mixed, cache_keys, cache_values)


def solution(mesh):
    in_specs = (
        P(("dp", "cache"), None),
        P("dp"),
        P(("dp", "cache")),
        P(),
        P(("dp", "cache"), None),
        P(("dp", "cache"), None),
        P(),
        P(("dp", "cache"), None),
        P(("dp", "cache"), None),
        P(("dp", "cache"), None, None),
        P(("dp", "cache"), None, None),
    )
    out_specs = (P(("dp", "cache"), None), P(("dp", "cache"), None), P(("dp", "cache"), None))
    return jax.shard_map(
        per_device, mesh=mesh, in_specs=in_specs, out_specs=out_specs, check_vma=False
    )
```

profile of v0, /device:TPU:33, one launch (start us, length us, event | category | flops | bytes accessed | tf_op | source)
XLA Modules:
  0.0 1172.3 jit_solution(6544326137829235413)
XLA Ops:
  7.2 0.7 all-gather.7.cloned.1.call-update
  7.9 0.7 all-gather.5.cloned.1.call-update
  8.7 0.8 copy.45
  9.7 0.8 subtract_convert_fusion.1
  10.9 0.7 broadcast_multiply_fusion
  11.9 1.8 reduce-window.6
  13.7 0.3 slice_reduce_fusion
  14.2 3.4 scatter_custom_fusion
  17.6 1.3 fusion.18
  18.9 0.9 compare_and_fusion
  19.8 310.8 %all-gather.7.cloned.1.call-done = bf16[128,10,2560]{2,1,0:T(8,128)(2,1)} async-done(((bf16[1,10,2560]{2,1,0:T(8,128)(2,1)}), bf16[128,10,2560]{2,1,0:T(8,128)(2,1)}) %all-gather.7.cloned.1.call-update) | async-done | bytes 6553616 | tf_op jit(solution)/shard_map/all_gather | solution.py:76
  330.6 12.8 %reshape.368 = bf16[1280,2560]{1,0:T(8,128)(2,1)} reshape(bf16[128,10,2560]{2,1,0:T(8,128)(2,1)} %all-gather.7.cloned.1.call-done) | data formatting | bytes 13107200
  343.4 308.3 %all-gather.5.cloned.1.call-done = bf16[128,20,1792]{2,1,0:T(8,128)(2,1)} async-done(((bf16[1,20,1792]{2,1,0:T(8,128)(2,1)}), bf16[128,20,1792]{2,1,0:T(8,128)(2,1)}) %all-gather.5.cloned.1.call-update) | async-done | bytes 9175056 | tf_op jit(solution)/shard_map/all_gather | solution.py:75
  651.7 13.2 %reshape.366 = bf16[2560,1792]{1,0:T(8,128)(2,1)} reshape(bf16[128,20,1792]{2,1,0:T(8,128)(2,1)} %all-gather.5.cloned.1.call-done) | data formatting | bytes 18350080
  664.9 5.0 fusion.30
  669.9 0.6 slice.95
  670.6 23.6 %all_gather.13 = bf16[1024,256]{1,0:T(8,128)(2,1)S(1)} all-gather(bf16[128,256]{1,0:T(8,128)(2,1)} %slice.95), channel_id=1, replica_groups=mesh['dp'=16,'cache'=8] {'cache'}, dimensions={0}, use_global_device_ids=true | all-gather | bytes 589824 | tf_op jit(solution)/shard_map/all_gather | solution.py:87
  694.5 0.3 multiply_subtract_fusion
  695.1 21.1 %all_gather.14 = bf16[1024,256]{0,1:T(8,128)(2,1)S(1)} all-gather(bf16[128,256]{0,1:T(8,128)(2,1)S(1)} %bitcast.117), channel_id=1, replica_groups=mesh['dp'=16,'cache'=8] {'cache'}, dimensions={0}, use_global_device_ids=true | all-gather | bytes 589824 | tf_op jit(solution)/shard_map/all_gather | solution.py:86
  716.2 0.2 copy.38
  716.6 1.0 fusion.5
  717.6 1.1 fusion.8
  718.7 1.1 fusion.27
  719.9 1.2 slice-done.1
  721.0 1.1 multiply_reduce_fusion.1
  722.4 6.3 gather_fusion.1
  728.8 7.8 broadcast_in_dim.35
  736.5 136.7 %all_to_all.25 = bf16[128,16,2560]{2,1,0:T(8,128)(2,1)S(1)} all-to-all(bf16[128,16,2560]{2,1,0:T(8,128)(2,1)} %bitcast.107), channel_id=1, replica_groups=mesh['dp'=16,'cache'=8] {'dp','cache'}, dimensions={0} | all-to-all | bytes 20971520 | tf_op jit(solution)/shard_map/all_to_all | solution.py:130
  873.3 21.6 %fusion.2 = f32[2048,1536]{1,0:T(8,128)} fusion(bf16[2048,2560]{1,0:T(8,128)(2,1)S(1)} %bitcast.110, bf16[1,2560,1536]{2,1,0:T(8,128)(2,1)} %param.20), kind=kOutput, calls=%fused_computation.13 | convolution fusion | flops 16106127360 | bytes 30932992 | tf_op jit(solution)/shard_map/dot_general | solution.py:40
  894.9 17.3 %convolution_convert_fusion = bf16[2048,2560]{1,0:T(8,128)(2,1)} fusion(bf16[1,768,2560]{2,1,0:T(8,128)(2,1)S(1)} %copy-done.5, f32[2048,1536]{1,0:T(8,128)} %fusion.2), kind=kOutput, calls=%fused_computation.7 | convolution fusion | flops 8067743744 | bytes 27000832 | tf_op jit(solution)/shard_map/dot_general | solution.py:44
  912.2 12.0 %all-to-all-start.1 = ((bf16[128,16,2560]{2,1,0:T(8,128)(2,1)}), bf16[128,16,2560]{2,1,0:T(8,128)(2,1)}, u32[]{:S(2)}, u32[]{:S(2)}) async-start(bf16[128,16,2560]{2,1,0:T(8,128)(2,1)} %bitcast.109), calls=%async_computation.1 | async-start | bytes 20971520 | tf_op jit(solution)/shard_map/all_to_all | solution.py:140
  924.4 0.7 convert_element_type.104
  925.1 141.6 %all-to-all-done.1 = bf16[128,16,2560]{2,1,0:T(8,128)(2,1)} async-done(((bf16[128,16,2560]{2,1,0:T(8,128)(2,1)}), bf16[128,16,2560]{2,1,0:T(8,128)(2,1)}, u32[]{:S(2)}, u32[]{:S(2)}) %all-to-all-start.1) | async-done | bytes 10485792 | tf_op jit(solution)/shard_map/all_to_all | solution.py:140
  1066.7 19.8 %all-to-all-start.3 = ((bf16[8,16,256]{2,1,0:T(8,128)(2,1)}), bf16[8,16,256]{2,1,0:T(8,128)(2,1)S(1)}, u32[]{:S(2)}, u32[]{:S(2)}) async-start(bf16[8,16,256]{2,1,0:T(8,128)(2,1)} %convert_element_type.104), calls=%async_computation.3 | async-start | bytes 131072 | tf_op jit(solution)/shard_map/all_to_all | solution.py:157
  1086.5 14.1 %convert.14 = f32[64,2,16,2560]{3,2,1,0:T(8,128)} convert(bf16[64,2,16,2560]{3,2,1,0:T(8,128)(2,1)} %bitcast.24) | non-fusion elementwise | flops 5242880 | bytes 31457280 | tf_op jit(solution)/shard_map/convert_element_type | solution.py:143
  1100.5 11.1 fusion.1
  1111.6 11.5 gather_fusion.2
  1123.1 7.8 reshape.307
  1130.9 8.0 multiply_reduce_fusion
  1139.0 5.2 all-to-all-start.4
  1144.1 1.0 add_convert_fusion
  1145.1 4.2 all-to-all-done.4
  1149.3 3.5 all-to-all-start.2
  1153.1 1.0 gather_fusion
  1154.1 1.6 scatter_custom_fusion.2
  1155.7 1.6 scatter_custom_fusion.3
  1157.3 5.8 all-to-all-done.2
  1163.1 2.4 scatter_custom_fusion.1
  (54 shorter events, 2.5 us)
Async XLA Ops:
  7.2 323.5 %all-gather.7.cloned.1.call-start = ((), (), s32[]{:S(2)}) async-start(), calls=%async_computation.6 | async-start | bytes 10567680 | tf_op jit(solution)/shard_map/all_gather | solution.py:76
  7.9 643.8 %all-gather.5.cloned.1.call-start = ((), (), s32[]{:S(2)}) async-start(), calls=%async_computation.5 | async-start | bytes 11096064 | tf_op jit(solution)/shard_map/all_gather | solution.py:75
  343.4 321.4 %copy-start.1 = (bf16[128,2560]{1,0:T(8,128)(2,1)S(1)}, bf16[128,2560]{1,0:T(8,128)(2,1)}, u32[]{:S(2)}) copy-start(bf16[128,2560]{1,0:T(8,128)(2,1)} %param.11) | copy-start | bytes 1966084
  343.4 321.4 %copy-start.2 = (f32[2560]{0:T(1024)S(1)}, f32[2560]{0:T(1024)}, u32[]{:S(2)}) copy-start(f32[2560]{0:T(1024)} %param.14) | copy-start | bytes 30724
  717.6 2.3 slice-start
  718.7 2.3 slice-start.1
  721.0 1.1 copy-start.3
  873.3 21.6 %copy-start.5 = (bf16[1,768,2560]{2,1,0:T(8,128)(2,1)S(1)}, bf16[1,768,2560]{2,1,0:T(8,128)(2,1)}, u32[]{:S(2)}) copy-start(bf16[1,768,2560]{2,1,0:T(8,128)(2,1)} %param.21) | copy-start | bytes 11796484
  912.2 12.1 %copy-start.4 = (f32[128,6]{0,1:T(8,128)S(1)}, f32[128,6]{0,1:T(8,128)}, u32[]{:S(2)}) copy-start(f32[128,6]{0,1:T(8,128)} %param.19) | copy-start | bytes 9220
  912.2 154.5 %all-to-all-start.1 = ((bf16[128,16,2560]{2,1,0:T(8,128)(2,1)}), bf16[128,16,2560]{2,1,0:T(8,128)(2,1)}, u32[]{:S(2)}, u32[]{:S(2)}) async-start(bf16[128,16,2560]{2,1,0:T(8,128)(2,1)} %bitcast.109), calls=%async_computation.1 | async-start | bytes 20971520 | tf_op jit(solution)/shard_map/all_to_all | solution.py:140
  1066.7 72.3 %all-to-all-start.3 = ((bf16[8,16,256]{2,1,0:T(8,128)(2,1)}), bf16[8,16,256]{2,1,0:T(8,128)(2,1)S(1)}, u32[]{:S(2)}, u32[]{:S(2)}) async-start(bf16[8,16,256]{2,1,0:T(8,128)(2,1)} %convert_element_type.104), calls=%async_computation.3 | async-start | bytes 131072 | tf_op jit(solution)/shard_map/all_to_all | solution.py:157
  1130.9 22.1 %copy-start = (s32[1024]{0:T(1024)S(1)}, s32[1024]{0:T(1024)}, u32[]{:S(2)}) copy-start(s32[1024]{0:T(1024)} %param.12) | copy-start | bytes 12292
  1139.0 10.4 all-to-all-start.4
  1149.3 13.7 %all-to-all-start.2 = ((bf16[8,16,2560]{2,1,0:T(8,128)(2,1)}), bf16[8,16,2560]{2,1,0:T(8,128)(2,1)S(1)}, u32[]{:S(2)}, u32[]{:S(2)}) async-start(bf16[8,16,2560]{2,1,0:T(8,128)(2,1)} %bitcast.26), calls=%async_computation.2 | async-start | bytes 1310720 | tf_op jit(solution)/shard_map/all_to_all | solution.py:156
Sparse Core Ops, SparseCore 0:
  9.7 320.9 all-gather.6
  332.3 319.3 all-gather.4
where the time goes:
time: 1180 us; the launch traced here: 1170 us
  waiting for transfers between devices  772 us (65%)
  blocking collectives  181 us (15%)
  local copies, waits for them, and re-layouts  74.5 us (6%)
  matrix products  47.2 us (4%)
  other arithmetic  42 us (4%)
  starting transfers between devices  40.6 us (3%)
  between operations  14.4 us (1%)
    all_gather x1, waiting for transfers between devices, per_device(): lax.all_gather(w_out, ('dp', 'cache'), axis=0, tiled=True)  311 us
    all_gather x1, waiting for transfers between devices, per_device(): lax.all_gather(w_qkv, ('dp', 'cache'), axis=0, tiled=True)  308 us
    all_to_all x1, waiting for transfers between devices, per_device(): lax.all_to_all(partial_value, ('dp', 'cache'), split_axis=0, concat_axis=...  142 us
    all_to_all x1, blocking collectives, per_device(): lax.all_to_all(jnp.repeat(outgoing, 2, axis=0), ('dp', 'cache'), split_ax...  137 us
    unnamed x20, local copies, waits for them, and re-layouts  28.1 us
  transfers between devices with their start and end apart: 6, of which 5 were waited for; matrix products, arithmetic and copies ran while one was open for 7% of the time, Pallas kernels for 0%

commit v1 on v0

--- a/solution.py
+++ b/solution.py
@@ -72,7 +72,12 @@
     position = my_place - prompt_start
     normed = rms_scaled(hidden_in, attn_gain)
     full_qkv, full_out = (
-        lax.all_gather(w_qkv, ("dp", "cache"), axis=0, tiled=True),
+        jnp.concatenate(
+            lax.all_to_all(
+                jnp.stack([w_qkv] * lax.axis_size(("dp", "cache"))), ("dp", "cache"), 0, 0
+            ),
+            axis=0,
+        ),
         lax.all_gather(w_out, ("dp", "cache"), axis=0, tiled=True),
     )
     projected = jnp.dot(normed, full_qkv, preferred_element_type=jnp.float32)

time: 1180 us -> 899 us (0.76)
  waiting for transfers between devices: 772 us -> 481 us
    all_gather x1 -> x0, waiting for transfers between devices: 308 us -> none  [per_device(): lax.all_gather(w_qkv, ('dp', 'cache'), axis=0, tiled=True)]
    all_to_all x0 -> x1, waiting for transfers between devices: none -> 149 us  [per_device(): lax.all_to_all(jnp.stack([w_qkv] * lax.axis_size(('dp', 'cache'))), ('dp'...]
    all_gather x1, waiting for transfers between devices: 311 us -> 180 us  [per_device(): lax.all_gather(w_out, ('dp', 'cache'), axis=0, tiled=True)]
    unnamed x20 -> x21, local copies, waits for them, and re-layouts: 28.1 us -> 13.1 us
    reshape x0 -> x1, local copies, waits for them, and re-layouts: none -> 13.2 us  [per_device(): jnp.concatenate(lax.all_to_all(jnp.stack([w_qkv] * lax.axis_size(('dp', '...]
  transfers between devices with their start and end apart: 6 -> 6, of which waited for: 5 -> 5; matrix products, arithmetic and copies ran while one was open for 7% -> 11% of each run, Pallas kernels for 0% -> 0%
where the time goes in v1:
time: 899 us; the launch traced here: 893 us
  waiting for transfers between devices  481 us (54%)
  blocking collectives  189 us (21%)
  local copies, waits for them, and re-layouts  78.4 us (9%)
  matrix products  50.2 us (6%)
  starting transfers between devices  40.4 us (4%)
  other arithmetic  38.8 us (4%)
  between operations  14.6 us (2%)
    all_gather x1, waiting for transfers between devices, per_device(): lax.all_gather(w_out, ('dp', 'cache'), axis=0, tiled=True)  180 us
    all_to_all x1, waiting for transfers between devices, per_device(): lax.all_to_all(jnp.stack([w_qkv] * lax.axis_size(('dp', 'cache'))), ('dp'...  149 us
    all_to_all x1, waiting for transfers between devices, per_device(): lax.all_to_all(partial_value, ('dp', 'cache'), split_axis=0, concat_axis=...  142 us
    all_to_all x1, blocking collectives, per_device(): lax.all_to_all(jnp.repeat(outgoing, 2, axis=0), ('dp', 'cache'), split_ax...  133 us
    all_gather x1, blocking collectives, per_device(): value_piece = lax.all_gather(values_here, 'cache', axis=0, tiled=True)  30.3 us
    all_gather x1, blocking collectives, per_device(): key_piece = lax.all_gather(keys_here, 'cache', axis=0, tiled=True)  25.3 us
    dot_general x1, matrix products, expert_half(): joined = jnp.dot(flat_rows, gate_up, preferred_element_type=jnp.float32)  21.6 us
  transfers between devices with their start and end apart: 6, of which 5 were waited for; matrix products, arithmetic and copies ran while one was open for 11% of the time, Pallas kernels for 0%

profile of v1, /device:TPU:33, one launch (start us, length us, event | category | flops | bytes accessed | tf_op | source)
XLA Modules:
  0.0 892.6 jit_solution(5542672520479882659)
XLA Ops:
  7.2 0.7 all-gather.3.cloned.1.call-update
  7.9 5.7 stack.2
  13.6 10.9 %all-to-all-start = ((bf16[128,20,1792]{2,1,0:T(8,128)(2,1)}), bf16[128,20,1792]{2,1,0:T(8,128)(2,1)}, u32[]{:S(2)}, u32[]{:S(2)}) async-start(bf16[128,20,1792]{2,1,0:T(8,128)(2,1)} %stack.2), calls=%async_computation | async-start | bytes 22020096 | tf_op jit(solution)/shard_map/all_to_all | solution.py:76
  25.1 0.2 multiply_cosine_fusion
  25.8 1.8 reduce-window.6
  27.6 0.3 slice_reduce_fusion
  28.1 3.4 scatter_custom_fusion
  31.5 0.2 fusion.18
  31.7 0.2 compare_and_fusion
  31.9 148.7 %all-to-all-done = bf16[128,20,1792]{2,1,0:T(8,128)(2,1)} async-done(((bf16[128,20,1792]{2,1,0:T(8,128)(2,1)}), bf16[128,20,1792]{2,1,0:T(8,128)(2,1)}, u32[]{:S(2)}, u32[]{:S(2)}) %all-to-all-start) | async-done | bytes 9175072 | tf_op jit(solution)/shard_map/all_to_all | solution.py:76
  180.6 13.2 %reshape.297 = bf16[2560,1792]{1,0:T(8,128)(2,1)} reshape(bf16[128,20,1792]{2,1,0:T(8,128)(2,1)} %all-to-all-done) | data formatting | bytes 18350080 | tf_op jit(solution)/shard_map/reshape | solution.py:75
  193.8 5.1 fusion.30
  198.9 0.6 slice.95
  199.6 30.3 %all_gather.9 = bf16[1024,256]{1,0:T(8,128)(2,1)S(1)} all-gather(bf16[128,256]{1,0:T(8,128)(2,1)} %slice.95), channel_id=1, replica_groups=mesh['dp'=16,'cache'=8] {'cache'}, dimensions={0}, use_global_device_ids=true | all-gather | bytes 589824 | tf_op jit(solution)/shard_map/all_gather | solution.py:92
  229.9 0.2 copy.53
  230.2 0.3 multiply_subtract_fusion
  230.5 0.2 maximum_convert_fusion
  230.8 0.2 copy.38
  231.2 25.3 %all_gather.10 = bf16[1024,256]{0,1:T(8,128)(2,1)S(1)} all-gather(bf16[128,256]{0,1:T(8,128)(2,1)S(1)} %bitcast.114), channel_id=1, replica_groups=mesh['dp'=16,'cache'=8] {'cache'}, dimensions={0}, use_global_device_ids=true | all-gather | bytes 589824 | tf_op jit(solution)/shard_map/all_gather | solution.py:91
  256.5 1.0 fusion.5
  257.5 1.1 fusion.8
  258.6 1.2 fusion.27
  259.8 180.4 %all-gather.3.cloned.1.call-done = bf16[128,10,2560]{2,1,0:T(8,128)(2,1)} async-done(((bf16[1,10,2560]{2,1,0:T(8,128)(2,1)}), bf16[128,10,2560]{2,1,0:T(8,128)(2,1)}) %all-gather.3.cloned.1.call-update) | async-done | bytes 6553616 | tf_op jit(solution)/shard_map/all_gather | solution.py:81
  440.2 12.8 %reshape.372 = bf16[1280,2560]{1,0:T(8,128)(2,1)} reshape(bf16[128,10,2560]{2,1,0:T(8,128)(2,1)} %all-gather.3.cloned.1.call-done) | data formatting | bytes 13107200
  453.0 4.0 multiply_reduce_fusion.1
  457.3 6.3 gather_fusion.1
  463.6 7.8 broadcast_in_dim.35
  471.4 133.0 %all_to_all.30 = bf16[128,16,2560]{2,1,0:T(8,128)(2,1)S(1)} all-to-all(bf16[128,16,2560]{2,1,0:T(8,128)(2,1)} %bitcast.104), channel_id=1, replica_groups=mesh['dp'=16,'cache'=8] {'dp','cache'}, dimensions={0} | all-to-all | bytes 20971520 | tf_op jit(solution)/shard_map/all_to_all | solution.py:135
  604.4 21.6 %fusion.2 = f32[2048,1536]{1,0:T(8,128)} fusion(bf16[2048,2560]{1,0:T(8,128)(2,1)S(1)} %bitcast.107, bf16[1,2560,1536]{2,1,0:T(8,128)(2,1)} %param.20), kind=kOutput, calls=%fused_computation.13 | convolution fusion | flops 16106127360 | bytes 30932992 | tf_op jit(solution)/shard_map/dot_general | solution.py:40
  626.0 17.3 %convolution_convert_fusion = bf16[2048,2560]{1,0:T(8,128)(2,1)} fusion(bf16[1,768,2560]{2,1,0:T(8,128)(2,1)S(1)} %copy-done.8, f32[2048,1536]{1,0:T(8,128)} %fusion.2), kind=kOutput, calls=%fused_computation.7 | convolution fusion | flops 8067743744 | bytes 27000832 | tf_op jit(solution)/shard_map/dot_general | solution.py:44
  643.3 10.4 %all-to-all-start.2 = ((bf16[128,16,2560]{2,1,0:T(8,128)(2,1)}), bf16[128,16,2560]{2,1,0:T(8,128)(2,1)}, u32[]{:S(2)}, u32[]{:S(2)}) async-start(bf16[128,16,2560]{2,1,0:T(8,128)(2,1)} %bitcast.106), calls=%async_computation.2 | async-start | bytes 20971520 | tf_op jit(solution)/shard_map/all_to_all | solution.py:145
  653.9 0.7 convert_element_type.104
  654.6 141.6 %all-to-all-done.2 = bf16[128,16,2560]{2,1,0:T(8,128)(2,1)} async-done(((bf16[128,16,2560]{2,1,0:T(8,128)(2,1)}), bf16[128,16,2560]{2,1,0:T(8,128)(2,1)}, u32[]{:S(2)}, u32[]{:S(2)}) %all-to-all-start.2) | async-done | bytes 10485792 | tf_op jit(solution)/shard_map/all_to_all | solution.py:145
  796.2 10.3 %all-to-all-start.4 = ((bf16[8,16,256]{2,1,0:T(8,128)(2,1)}), bf16[8,16,256]{2,1,0:T(8,128)(2,1)S(1)}, u32[]{:S(2)}, u32[]{:S(2)}) async-start(bf16[8,16,256]{2,1,0:T(8,128)(2,1)} %convert_element_type.104), calls=%async_computation.4 | async-start | bytes 131072 | tf_op jit(solution)/shard_map/all_to_all | solution.py:162
  806.6 14.1 %convert.14 = f32[64,2,16,2560]{3,2,1,0:T(8,128)} convert(bf16[64,2,16,2560]{3,2,1,0:T(8,128)(2,1)} %bitcast.23) | non-fusion elementwise | flops 5242880 | bytes 31457280 | tf_op jit(solution)/shard_map/convert_element_type | solution.py:148
  820.6 11.1 %fusion.1 = bf16[64,1,16,2560]{3,2,0,1:T(8,128)(2,1)} fusion(f32[64,2,16,2560]{3,2,1,0:T(8,128)} %convert.14), kind=kLoop, calls=%fused_computation.10 | loop fusion | flops 5242880 | bytes 26214400 | tf_op jit(solution)/shard_map/convert_element_type | solution.py:149
  831.7 11.5 %gather_fusion.2 = bf16[768,2560]{1,0:T(8,128)(2,1)} fusion(bf16[1024,2560]{1,0:T(8,128)(2,1)} %bitcast.103, s32[1024]{0:T(1024)S(1)} %pad_clamp_fusion), kind=kCustom, calls=%fused_computation.2 | custom fusion | bytes 7867392 | tf_op jit(solution)/shard_map/gather | solution.py:150
  843.2 7.8 reshape.313
  851.0 8.0 multiply_reduce_fusion
  859.1 5.2 all-to-all-start.5
  864.2 1.0 add_convert_fusion
  865.2 4.2 all-to-all-done.5
  869.4 3.5 all-to-all-start.3
  873.1 1.0 gather_fusion
  874.1 1.6 scatter_custom_fusion.2
  875.7 1.6 scatter_custom_fusion.3
  877.4 5.8 all-to-all-done.3
  883.2 2.4 scatter_custom_fusion.1
  (55 shorter events, 2.1 us)
Async XLA Ops:
  7.2 433.0 %all-gather.3.cloned.1.call-start = ((), (), s32[]{:S(2)}) async-start(), calls=%async_computation.6 | async-start | bytes 10567680 | tf_op jit(solution)/shard_map/all_gather | solution.py:81
  13.6 11.0 %copy-start.4 = (s32[128,6]{0,1:T(8,128)S(1)}, s32[128,6]{0,1:T(8,128)}, u32[]{:S(2)}) copy-start(s32[128,6]{0,1:T(8,128)} %param.18) | copy-start | bytes 9220
  13.6 11.4 %copy-start = (s32[1024]{0:T(1024)S(1)}, s32[1024]{0:T(1024)}, u32[]{:S(2)}) copy-start(s32[1024]{0:T(1024)} %param.12) | copy-start | bytes 12292
  13.6 11.4 %copy-start.7 = (s32[128]{0:T(128)S(1)}, s32[128]{0:T(128)}, u32[]{:S(2)}) copy-start(s32[128]{0:T(128)} %param.13) | copy-start | bytes 1540
  13.6 17.8 %copy-start.2 = (bf16[128,2560]{1,0:T(8,128)(2,1)S(1)}, bf16[128,2560]{1,0:T(8,128)(2,1)}, u32[]{:S(2)}) copy-start(bf16[128,2560]{1,0:T(8,128)(2,1)} %param.11) | copy-start | bytes 1966084
  13.6 167.0 %all-to-all-start = ((bf16[128,20,1792]{2,1,0:T(8,128)(2,1)}), bf16[128,20,1792]{2,1,0:T(8,128)(2,1)}, u32[]{:S(2)}, u32[]{:S(2)}) async-start(bf16[128,20,1792]{2,1,0:T(8,128)(2,1)} %stack.2), calls=%async_computation | async-start | bytes 22020096 | tf_op jit(solution)/shard_map/all_to_all | solution.py:76
  31.9 161.9 %copy-start.3 = (f32[2560]{0:T(1024)S(1)}, f32[2560]{0:T(1024)}, u32[]{:S(2)}) copy-start(f32[2560]{0:T(1024)} %param.14) | copy-start | bytes 30724
  453.0 4.0 copy-start.5
  604.4 21.6 %copy-start.8 = (bf16[1,768,2560]{2,1,0:T(8,128)(2,1)S(1)}, bf16[1,768,2560]{2,1,0:T(8,128)(2,1)}, u32[]{:S(2)}) copy-start(bf16[1,768,2560]{2,1,0:T(8,128)(2,1)} %param.21) | copy-start | bytes 11796484
  643.3 10.4 %copy-start.6 = (f32[128,6]{0,1:T(8,128)S(1)}, f32[128,6]{0,1:T(8,128)}, u32[]{:S(2)}) copy-start(f32[128,6]{0,1:T(8,128)} %param.19) | copy-start | bytes 9220
  643.3 152.9 %all-to-all-start.2 = ((bf16[128,16,2560]{2,1,0:T(8,128)(2,1)}), bf16[128,16,2560]{2,1,0:T(8,128)(2,1)}, u32[]{:S(2)}, u32[]{:S(2)}) async-start(bf16[128,16,2560]{2,1,0:T(8,128)(2,1)} %bitcast.106), calls=%async_computation.2 | async-start | bytes 20971520 | tf_op jit(solution)/shard_map/all_to_all | solution.py:145
  796.2 62.8 %all-to-all-start.4 = ((bf16[8,16,256]{2,1,0:T(8,128)(2,1)}), bf16[8,16,256]{2,1,0:T(8,128)(2,1)S(1)}, u32[]{:S(2)}, u32[]{:S(2)}) async-start(bf16[8,16,256]{2,1,0:T(8,128)(2,1)} %convert_element_type.104), calls=%async_computation.4 | async-start | bytes 131072 | tf_op jit(solution)/shard_map/all_to_all | solution.py:162
  851.0 22.1 %copy-start.1 = (s32[1024]{0:T(1024)S(1)}, s32[1024]{0:T(1024)}, u32[]{:S(2)}) copy-start(s32[1024]{0:T(1024)} %param.12) | copy-start | bytes 12292
  859.1 10.4 %all-to-all-start.5 = ((bf16[8,16,256]{2,1,0:T(8,128)(2,1)}), bf16[8,16,256]{2,1,0:T(8,128)(2,1)S(1)}, u32[]{:S(2)}, u32[]{:S(2)}) async-start(bf16[8,16,256]{2,1,0:T(8,128)(2,1)} %bitcast.28), calls=%async_computation.5 | async-start | bytes 131072 | tf_op jit(solution)/shard_map/all_to_all | solution.py:163
  869.4 13.7 %all-to-all-start.3 = ((bf16[8,16,2560]{2,1,0:T(8,128)(2,1)}), bf16[8,16,2560]{2,1,0:T(8,128)(2,1)S(1)}, u32[]{:S(2)}, u32[]{:S(2)}) async-start(bf16[8,16,2560]{2,1,0:T(8,128)(2,1)} %bitcast.25), calls=%async_computation.3 | async-start | bytes 1310720 | tf_op jit(solution)/shard_map/all_to_all | solution.py:161
Sparse Core Ops, SparseCore 0:
  9.7 430.4 all-gather.2
